TPU v7x, 128 devices: a whole 4x4x4 slice. The times are simulated.
128 devices in a mesh: dp: 8 (over z, core), fsdp: 16 (over x, y).
Axes of the slice: x: 4, y: 4, z: 4, core: 2. Of those that a mesh axis runs over, the one named last changes fastest.
Arguments:
- gate_act: bfloat16 [4096, 14848], P('fsdp', 'dp'), may hold values from -6 to 6
- up_act: bfloat16 [4096, 14848], P('fsdp', 'dp'), may hold values from -6 to 6
- out_grad: bfloat16 [4096, 4096], P('fsdp'), may hold values from -6 to 6
- master_old: float32 [8, 2176, 4096], P('dp', 'fsdp'), may hold values from -0.046875 to 0.046875
- moment1_old: float32 [8, 2176, 4096], P('dp', 'fsdp'), may hold values from -4 to 4
- moment2_old: float32 [8, 2176, 4096], P('dp', 'fsdp'), may hold values from 0.02 to 4
- old_bounds: int32 [8, 17], P('dp'), may hold values from 0 to 1856, as said below
- new_bounds: int32 [8, 16], P('dp'), may hold values from 0 to 1856, as said below
- rank_map: int32 [8, 16], P('dp'), may hold values from 0 to 15, as said below
Outputs:
- mlp_out: float32 [4096, 4096], P('fsdp', 'dp')
- master_new: float32 [8, 2176, 4096], P('dp', 'fsdp')
- moment1_new: float32 [8, 2176, 4096], P('dp', 'fsdp')
- moment2_new: float32 [8, 2176, 4096], P('dp', 'fsdp')
Inputs may be any that keep to these rules, and one draw needn't show every extreme that they name: Each row of old_bounds starts at 0, ends at 1856 and never falls; each position's rows fit its 136 slots. Each row of new_bounds starts at 0, ends at 1856 and never falls; each rank's rows fit 136 slots. In every block a position's new rows lie within its old rows and at most 58 rows of each of its two neighbours. `rank_map`: in each block's row exactly one position, one of the two middle ones, has rank 16 - 1 and owns nothing; the others hold the ranks 0 to 14 in position order.
All inputs are finite; a program needn't handle non-finite values.
Results may differ from a plain program's by a relative error of at most 0.012.
Values may be sent and summed in bfloat16 or wider, within the bound.
A program may use at most 192 MiB of HBM per device.

v0:
```python
import math
import jax
import jax.numpy as jnp
from jax import lax
from jax.sharding import PartitionSpec as P


def passed_along(value, axis, steps):
    count = lax.axis_size(axis)
    leading, last = (max(0, -steps), min(count, count - steps))
    return lax.ppermute(value, axis, [(source, source + steps) for source in range(leading, last)])


def pick_entry(table, index):
    return jnp.sum(jnp.where(jnp.arange(table.shape[0]) == index, table, jnp.zeros_like(table)))


def migrate(stacked, moved_rows, my_old_start, my_old_count, my_new_start, my_new_count):
    slot_rows = stacked.shape[1]
    prefix = stacked[:, :moved_rows]
    padded = jnp.concatenate(
        [jnp.zeros((3, moved_rows, stacked.shape[2]), stacked.dtype), stacked], axis=1
    )
    suffix = lax.dynamic_slice_in_dim(padded, my_old_count, moved_rows, 1)
    from_right = passed_along(prefix.astype(jnp.bfloat16), "fsdp", -1).astype(prefix.dtype)
    from_left = passed_along(suffix.astype(jnp.bfloat16), "fsdp", 1).astype(suffix.dtype)
    source = jnp.concatenate([from_left, stacked, from_right], axis=1)
    row_index = jnp.arange(slot_rows)
    global_row = my_new_start + row_index
    my_old_end = my_old_start + my_old_count
    index = (
        moved_rows
        + global_row
        - my_old_start
        + jnp.where(global_row >= my_old_end, slot_rows - my_old_count, 0)
    )
    index = jnp.clip(index, 0, 2 * moved_rows + slot_rows - 1)
    chosen = jnp.take(source, index, axis=1)
    return jnp.where((row_index < my_new_count)[None, :, None], chosen, jnp.zeros_like(chosen))


def block_product(hidden, weight_shard, table_start, table_count):
    slot_rows = weight_shard.shape[0]
    padded_hidden = jnp.concatenate(
        [hidden, jnp.zeros((hidden.shape[0], slot_rows), hidden.dtype)], axis=1
    )
    row_index = jnp.arange(slot_rows)[:, None]
    empty = jnp.zeros((hidden.shape[0], weight_shard.shape[1]), jnp.float32)
    piece = lax.all_gather(weight_shard, "fsdp", axis=0, tiled=True)
    shard_count = piece.shape[0] // slot_rows
    blocks = piece.reshape(shard_count, slot_rows, piece.shape[1])

    def one_shard(step, carry):
        start_col = pick_entry(table_start, step)
        live_rows = pick_entry(table_count, step)
        block = lax.dynamic_index_in_dim(blocks, step, 0, keepdims=False)
        block = jnp.where(row_index < live_rows, block, jnp.zeros_like(block))
        columns = lax.dynamic_slice_in_dim(padded_hidden, start_col, slot_rows, 1)
        return carry + jnp.dot(columns, block, preferred_element_type=jnp.float32)

    return lax.fori_loop(0, shard_count, one_shard, empty)


def local(
    gate_act,
    up_act,
    out_grad,
    master_old,
    moment1_old,
    moment2_old,
    old_bounds,
    new_bounds,
    rank_map,
):
    ranks_total = lax.axis_size("fsdp")
    my_position = lax.axis_index("fsdp")
    slot_rows = master_old.shape[1]
    token_rows = gate_act.shape[0]
    block_rows = gate_act.shape[1]
    base_rows = block_rows // ranks_total
    moved_rows = (base_rows + 1) // 2
    grad_scale = 1.0 / math.sqrt(token_rows * ranks_total)
    my_old_bounds = old_bounds[0]
    my_new_bounds = new_bounds[0]
    my_rank_map = rank_map[0]
    old_start = my_old_bounds[:-1]
    old_count = my_old_bounds[1:] - my_old_bounds[:-1]
    extended = jnp.concatenate([my_new_bounds, my_new_bounds[-1:]])
    extended_next = jnp.concatenate([extended[1:], extended[-1:]])
    owner_hit = my_rank_map[:, None] == jnp.arange(ranks_total + 1)[None, :]
    new_start = jnp.sum(jnp.where(owner_hit, extended[None, :], 0), axis=1)
    new_count = jnp.sum(jnp.where(owner_hit, extended_next[None, :], 0), axis=1) - new_start
    hidden = (jax.nn.silu(gate_act.astype(jnp.float32)) * up_act.astype(jnp.float32)).astype(
        jnp.bfloat16
    )
    stacked = jnp.stack([master_old[0], moment1_old[0], moment2_old[0]])
    moved = migrate(
        stacked,
        moved_rows,
        pick_entry(old_start, my_position),
        pick_entry(old_count, my_position),
        pick_entry(new_start, my_position),
        pick_entry(new_count, my_position),
    )
    weight_shard = moved[0].astype(jnp.bfloat16)
    block_part = block_product(hidden, weight_shard, new_start, new_count)
    mlp_out = lax.psum_scatter(
        block_part.astype(jnp.bfloat16), "dp", scatter_dimension=1, tiled=True
    ).astype(jnp.float32)
    row_index = jnp.arange(slot_rows * lax.axis_size("fsdp"))
    position = row_index // slot_rows
    within = row_index % slot_rows
    hit = position[:, None] == jnp.arange(ranks_total)[None, :]
    start_col = jnp.sum(jnp.where(hit, new_start[None, :], 0), axis=1)
    live_rows = jnp.sum(jnp.where(hit, new_count[None, :], 0), axis=1)
    column = jnp.clip(start_col + within, 0, block_rows - 1)
    chosen = jnp.take(hidden, column, axis=1)
    chosen = jnp.where((within < live_rows)[None, :], chosen, jnp.zeros_like(chosen))
    grad = (
        lax.psum_scatter(
            lax.dot_general(
                chosen, out_grad, (((0,), (0,)), ((), ())), preferred_element_type=jnp.float32
            ).astype(jnp.bfloat16),
            "fsdp",
            scatter_dimension=0,
            tiled=True,
        ).astype(jnp.float32)
        * grad_scale
    )
    first_next = 0.9 * moved[1] + 0.1 * grad
    second_next = 0.95 * moved[2] + 0.05 * grad * grad
    master_next = moved[0] - 0.001 * (first_next / (jnp.sqrt(second_next) + 1e-08) + 0.1 * moved[0])
    return (mlp_out, master_next[None], first_next[None], second_next[None])


def solution(mesh):
    placed = (
        P("fsdp", "dp"),
        P("fsdp", "dp"),
        P("fsdp", None),
        P("dp", "fsdp", None),
        P("dp", "fsdp", None),
        P("dp", "fsdp", None),
        P("dp", None),
        P("dp", None),
        P("dp", None),
    )
    return jax.shard_map(
        local,
        mesh=mesh,
        in_specs=placed,
        out_specs=(
            P("fsdp", "dp"),
            P("dp", "fsdp", None),
            P("dp", "fsdp", None),
            P("dp", "fsdp", None),
        ),
        check_vma=False,
    )
```

profile of v0, /device:TPU:0, one launch (start us, length us, event | category | flops | bytes accessed | tf_op | source)
XLA Modules:
  0.0 450.1 jit_solution(16102866951896543829)
XLA Ops:
  39.6 26.3 %collective-permute-done = bf16[3,58,4096]{2,1,0:T(8,128)(2,1)} collective-permute-done((bf16[3,58,4096]{2,1,0:T(8,128)(2,1)}, bf16[3,58,4096]{2,1,0:T(8,128)(2,1)}, u32[]{:S(2)}, u32[]{:S(2)}) %collective-permute-start) | collective-permute-done | bytes 1425440 | tf_op jit(solution)/shard_map/ppermute | solution.py:11
  75.1 23.1 %copy.39 = f32[3,252,4096]{2,0,1:T(4,128)} copy(f32[3,252,4096]{2,1,0:T(8,128)S(1)} %pad_maximum_fusion) | data formatting | bytes 24772608 | tf_op jit(solution)/shard_map/concatenate | solution.py:27
  98.2 17.2 %gather_fusion = f32[136,3,4096]{2,1,0:T(4,128)} fusion(f32[3,252,4096]{2,0,1:T(4,128)} %copy.39, s32[1024]{0:T(1024)S(1)} %pad_clamp_fusion.1), kind=kCustom, calls=%fused_computation | custom fusion | bytes 13369888 | tf_op jit(solution)/shard_map/jit(_take)/gather | solution.py:38
  115.4 12.2 %select_bitcast_fusion = f32[3,136,4096]{2,0,1:T(4,128)} fusion(f32[136,3,4096]{2,1,0:T(4,128)} %gather_fusion, pred[136]{0:T(512)(128)(4,1)S(1)} %iota_compare_fusion.2, pred[136]{0:T(512)(128)(4,1)S(1)} %compare_and_fusion.1), kind=kLoop, calls=%fused_computation.19 | loop fusion | flops 3342336 | bytes 13369616 | tf_op jit(solution)/shard_map/jit(_where)/select_n | solution.py:39
  127.7 16.3 %slice_multiply_fusion = (f32[1,136,4096]{2,0,1:T(1,128)}, f32[1,136,4096]{2,0,1:T(1,128)S(1)}, f32[1,136,4096]{2,0,1:T(1,128)}) fusion(f32[3,136,4096]{2,0,1:T(4,128)} %select_bitcast_fusion), kind=kLoop, calls=%fused_computation.30 | loop fusion | flops 557056 | bytes 13369344 | tf_op jit(solution)/shard_map/mul | solution.py:131
  149.9 7.7 %gather_fusion.1 = bf16[2176,256]{1,0:T(8,128)(2,1)} fusion(bf16[256,1856]{0,1:T(8,128)(2,1)S(1)} %fusion.20, s32[3072]{0:T(1024)S(1)} %pad_clamp_fusion), kind=kCustom, calls=%fused_computation.1 | custom fusion | bytes 2236928 | tf_op jit(solution)/shard_map/jit(_take)/gather | solution.py:117
  157.6 10.2 %convolution_convert_fusion = bf16[2176,4096]{1,0:T(8,128)(2,1)} fusion(bf16[256,4096]{1,0:T(8,128)(2,1)S(1)} %copy-done, bf16[2176,256]{1,0:T(8,128)(2,1)} %gather_fusion.1, pred[2176]{0:T(1024)(128)(4,1)S(1)} %fusion.32, pred[2176]{0:T(1024)(128)(4,1)S(1)} %compare_and_fusion), kind=kOutput, calls=%fused_computation.16 | convolution fusion | flops 4573429760 | bytes 21041408 | tf_op jit(solution)/shard_map/dot_general | solution.py:121
  168.0 98.5 %all-gather.2.cloned.1.call-done = bf16[2176,4096]{1,0:T(8,128)(2,1)} async-done(((bf16[136,4096]{1,0:T(8,128)(2,1)}), bf16[2176,4096]{1,0:T(8,128)(2,1)}) %all-gather.2.cloned.1.call-update) | async-done | bytes 17825808 | tf_op jit(solution)/shard_map/all_gather | solution.py:49
  266.5 137.3 %while.14 = (s32[]{:T(128)}, f32[256,4096]{1,0:T(8,128)}, s32[16]{0:T(128)S(1)}, bf16[256,1992]{0,1:T(8,128)(2,1)S(1)}, s32[16]{0:T(128)S(1)}, /*index=5*/bf16[1...) while((s32[]{:T(128)}, f32[256,4096]{1,0:T(8,128)}, s32[16]{0:T(128)S(1)}, ...), condition=%wide.region_9.10_spmd.clone, body=%wide.region_6.9_spmd.clone.sunk | while | flops 287867104 | bytes 9573797 | solution.py:61
  277.0 5.8 %convolution_add_fusion.2 = f32[256,4096]{1,0:T(8,128)} fusion(f32[256,4096]{1,0:T(8,128)} %get-tuple-element.267, pred[]{:T(512)S(6)} %compare.5, bf16[16,136,4096]{2,1,0:T(8,128)(2,1)} %get-tuple-element.280, s32[]{:T(128)} %get-tuple-element.266, pred[136]{0:T(512)(128)(4,1)S(1)} %compare_reduce_fusion.2, ...), kind=kOutput, calls=%fused_computation.3.clone.1 | convolution fusion | flops 287866880 | bytes 9573381 | tf_op jit(solution)/shard_map/while/body/eval_jaxpr/dot_general | solution.py:59
  286.1 5.4 %convolution_add_fusion.2 = f32[256,4096]{1,0:T(8,128)} fusion(f32[256,4096]{1,0:T(8,128)} %get-tuple-element.267, pred[]{:T(512)S(6)} %compare.5, bf16[16,136,4096]{2,1,0:T(8,128)(2,1)} %get-tuple-element.280, s32[]{:T(128)} %get-tuple-element.266, pred[136]{0:T(512)(128)(4,1)S(1)} %compare_reduce_fusion.2, ...), kind=kOutput, calls=%fused_computation.3.clone.1 | convolution fusion | flops 287866880 | bytes 9573381 | tf_op jit(solution)/shard_map/while/body/eval_jaxpr/dot_general | solution.py:59
  294.7 5.3 %convolution_add_fusion.2 = f32[256,4096]{1,0:T(8,128)} fusion(f32[256,4096]{1,0:T(8,128)} %get-tuple-element.267, pred[]{:T(512)S(6)} %compare.5, bf16[16,136,4096]{2,1,0:T(8,128)(2,1)} %get-tuple-element.280, s32[]{:T(128)} %get-tuple-element.266, pred[136]{0:T(512)(128)(4,1)S(1)} %compare_reduce_fusion.2, ...), kind=kOutput, calls=%fused_computation.3.clone.1 | convolution fusion | flops 287866880 | bytes 9573381 | tf_op jit(solution)/shard_map/while/body/eval_jaxpr/dot_general | solution.py:59
  303.3 5.5 %convolution_add_fusion.2 = f32[256,4096]{1,0:T(8,128)} fusion(f32[256,4096]{1,0:T(8,128)} %get-tuple-element.267, pred[]{:T(512)S(6)} %compare.5, bf16[16,136,4096]{2,1,0:T(8,128)(2,1)} %get-tuple-element.280, s32[]{:T(128)} %get-tuple-element.266, pred[136]{0:T(512)(128)(4,1)S(1)} %compare_reduce_fusion.2, ...), kind=kOutput, calls=%fused_computation.3.clone.1 | convolution fusion | flops 287866880 | bytes 9573381 | tf_op jit(solution)/shard_map/while/body/eval_jaxpr/dot_general | solution.py:59
  312.1 5.4 %convolution_add_fusion.2 = f32[256,4096]{1,0:T(8,128)} fusion(f32[256,4096]{1,0:T(8,128)} %get-tuple-element.267, pred[]{:T(512)S(6)} %compare.5, bf16[16,136,4096]{2,1,0:T(8,128)(2,1)} %get-tuple-element.280, s32[]{:T(128)} %get-tuple-element.266, pred[136]{0:T(512)(128)(4,1)S(1)} %compare_reduce_fusion.2, ...), kind=kOutput, calls=%fused_computation.3.clone.1 | convolution fusion | flops 287866880 | bytes 9573381 | tf_op jit(solution)/shard_map/while/body/eval_jaxpr/dot_general | solution.py:59
  320.7 5.4 %convolution_add_fusion.2 = f32[256,4096]{1,0:T(8,128)} fusion(f32[256,4096]{1,0:T(8,128)} %get-tuple-element.267, pred[]{:T(512)S(6)} %compare.5, bf16[16,136,4096]{2,1,0:T(8,128)(2,1)} %get-tuple-element.280, s32[]{:T(128)} %get-tuple-element.266, pred[136]{0:T(512)(128)(4,1)S(1)} %compare_reduce_fusion.2, ...), kind=kOutput, calls=%fused_computation.3.clone.1 | convolution fusion | flops 287866880 | bytes 9573381 | tf_op jit(solution)/shard_map/while/body/eval_jaxpr/dot_general | solution.py:59
  329.4 5.4 %convolution_add_fusion.2 = f32[256,4096]{1,0:T(8,128)} fusion(f32[256,4096]{1,0:T(8,128)} %get-tuple-element.267, pred[]{:T(512)S(6)} %compare.5, bf16[16,136,4096]{2,1,0:T(8,128)(2,1)} %get-tuple-element.280, s32[]{:T(128)} %get-tuple-element.266, pred[136]{0:T(512)(128)(4,1)S(1)} %compare_reduce_fusion.2, ...), kind=kOutput, calls=%fused_computation.3.clone.1 | convolution fusion | flops 287866880 | bytes 9573381 | tf_op jit(solution)/shard_map/while/body/eval_jaxpr/dot_general | solution.py:59
  338.1 5.4 %convolution_add_fusion.2 = f32[256,4096]{1,0:T(8,128)} fusion(f32[256,4096]{1,0:T(8,128)} %get-tuple-element.267, pred[]{:T(512)S(6)} %compare.5, bf16[16,136,4096]{2,1,0:T(8,128)(2,1)} %get-tuple-element.280, s32[]{:T(128)} %get-tuple-element.266, pred[136]{0:T(512)(128)(4,1)S(1)} %compare_reduce_fusion.2, ...), kind=kOutput, calls=%fused_computation.3.clone.1 | convolution fusion | flops 287866880 | bytes 9573381 | tf_op jit(solution)/shard_map/while/body/eval_jaxpr/dot_general | solution.py:59
  346.7 5.4 %convolution_add_fusion.2 = f32[256,4096]{1,0:T(8,128)} fusion(f32[256,4096]{1,0:T(8,128)} %get-tuple-element.267, pred[]{:T(512)S(6)} %compare.5, bf16[16,136,4096]{2,1,0:T(8,128)(2,1)} %get-tuple-element.280, s32[]{:T(128)} %get-tuple-element.266, pred[136]{0:T(512)(128)(4,1)S(1)} %compare_reduce_fusion.2, ...), kind=kOutput, calls=%fused_computation.3.clone.1 | convolution fusion | flops 287866880 | bytes 9573381 | tf_op jit(solution)/shard_map/while/body/eval_jaxpr/dot_general | solution.py:59
  364.0 5.3 %convolution_add_fusion.2 = f32[256,4096]{1,0:T(8,128)} fusion(f32[256,4096]{1,0:T(8,128)} %get-tuple-element.267, pred[]{:T(512)S(6)} %compare.5, bf16[16,136,4096]{2,1,0:T(8,128)(2,1)} %get-tuple-element.280, s32[]{:T(128)} %get-tuple-element.266, pred[136]{0:T(512)(128)(4,1)S(1)} %compare_reduce_fusion.2, ...), kind=kOutput, calls=%fused_computation.3.clone.1 | convolution fusion | flops 287866880 | bytes 9573381 | tf_op jit(solution)/shard_map/while/body/eval_jaxpr/dot_general | solution.py:59
  372.6 5.4 %convolution_add_fusion.2 = f32[256,4096]{1,0:T(8,128)} fusion(f32[256,4096]{1,0:T(8,128)} %get-tuple-element.267, pred[]{:T(512)S(6)} %compare.5, bf16[16,136,4096]{2,1,0:T(8,128)(2,1)} %get-tuple-element.280, s32[]{:T(128)} %get-tuple-element.266, pred[136]{0:T(512)(128)(4,1)S(1)} %compare_reduce_fusion.2, ...), kind=kOutput, calls=%fused_computation.3.clone.1 | convolution fusion | flops 287866880 | bytes 9573381 | tf_op jit(solution)/shard_map/while/body/eval_jaxpr/dot_general | solution.py:59
  381.2 5.4 %convolution_add_fusion.2 = f32[256,4096]{1,0:T(8,128)} fusion(f32[256,4096]{1,0:T(8,128)} %get-tuple-element.267, pred[]{:T(512)S(6)} %compare.5, bf16[16,136,4096]{2,1,0:T(8,128)(2,1)} %get-tuple-element.280, s32[]{:T(128)} %get-tuple-element.266, pred[136]{0:T(512)(128)(4,1)S(1)} %compare_reduce_fusion.2, ...), kind=kOutput, calls=%fused_computation.3.clone.1 | convolution fusion | flops 287866880 | bytes 9573381 | tf_op jit(solution)/shard_map/while/body/eval_jaxpr/dot_general | solution.py:59
  398.5 5.3 %convolution_add_fusion.2 = f32[256,4096]{1,0:T(8,128)} fusion(f32[256,4096]{1,0:T(8,128)} %get-tuple-element.267, pred[]{:T(512)S(6)} %compare.5, bf16[16,136,4096]{2,1,0:T(8,128)(2,1)} %get-tuple-element.280, s32[]{:T(128)} %get-tuple-element.266, pred[136]{0:T(512)(128)(4,1)S(1)} %compare_reduce_fusion.2, ...), kind=kOutput, calls=%fused_computation.3.clone.1 | convolution fusion | flops 287866880 | bytes 9573381 | tf_op jit(solution)/shard_map/while/body/eval_jaxpr/dot_general | solution.py:59
  407.7 12.8 %fusion.24 = (f32[1,136,4096]{2,1,0:T(8,128)}, f32[1,136,4096]{2,1,0:T(8,128)}, f32[1,136,4096]{2,1,0:T(8,128)}) fusion(bf16[136,4096]{1,0:T(8,128)(2,1)} %reduce-scatter.7.cloned.1.call-done, f32[1,136,4096]{2,0,1:T(1,128)} %get-tuple-element.204, f32[1,136,4096]{2,0,1:T(1,128)} %get-tuple-element.206, f32[1,136,4096]{2,0,1:T(1,128)} %copy-done.3), kind=kLoop, calls=%fused_computation.44 | loop fusion | flops 7798784 | bytes 14483456 | tf_op jit(solution)/shard_map/broadcast_in_dim | solution.py:133
  420.5 21.3 %reduce-scatter.5.cloned.1.call-done = bf16[256,512]{1,0:T(8,128)(2,1)} async-done(((bf16[256,4096]{1,0:T(8,128)(2,1)}), bf16[256,512]{1,0:T(8,128)(2,1)}) %reduce-scatter.5.cloned.1.call-update) | async-done | bytes 262160 | tf_op jit(solution)/shard_map/reduce_scatter | solution.py:107
  (84 shorter events, 84.8 us)
Async XLA Ops:
  7.2 150.4 %copy-start = (bf16[256,4096]{1,0:T(8,128)(2,1)S(1)}, bf16[256,4096]{1,0:T(8,128)(2,1)}, u32[]{:S(2)}) copy-start(bf16[256,4096]{1,0:T(8,128)(2,1)} %param.13) | copy-start | bytes 6291460
  7.2 259.3 %all-gather.2.cloned.1.call-start = ((), (), s32[]{:S(2)}) async-start(), calls=%async_computation.2 | async-start | bytes 18939904 | tf_op jit(solution)/shard_map/all_gather | solution.py:49
  18.3 3.4 copy-start.4
  28.4 37.5 %collective-permute-start = (bf16[3,58,4096]{2,1,0:T(8,128)(2,1)}, bf16[3,58,4096]{2,1,0:T(8,128)(2,1)}, u32[]{:S(2)}, u32[]{:S(2)}) collective-permute-start(bf16[3,58,4096]{2,1,0:T(8,128)(2,1)} %get-tuple-element.207), channel_id=1, source_target_pairs={{0,1},{1,2},{2,3},{3,4},{4,5},{5,6},{6,7},{7,8},{8,9},{9,10},{10,1... | collective-permute-start | bytes 4276232 | tf_op jit(solution)/shard_map/ppermute | solution.py:11
  33.2 38.1 %collective-permute-start.1 = (bf16[3,58,4096]{2,1,0:T(8,128)(2,1)}, bf16[3,58,4096]{2,1,0:T(8,128)(2,1)}, u32[]{:S(2)}, u32[]{:S(2)}) collective-permute-start(bf16[3,58,4096]{2,1,0:T(8,128)(2,1)} %get-tuple-element.208), channel_id=1, source_target_pairs={{1,0},{2,1},{3,2},{4,3},{5,4},{6,5},{7,6},{8,7},{9,8},{10,9},{11,1... | collective-permute-start | bytes 4276232 | tf_op jit(solution)/shard_map/ppermute | solution.py:11
  65.9 7.1 %copy-start.2 = (f32[3,136,4096]{2,1,0:T(8,128)S(1)}, f32[3,136,4096]{2,1,0:T(8,128)}, u32[]{:S(2)}) copy-start(f32[3,136,4096]{2,1,0:T(8,128)} %constant_dynamic-update-slice_fusion) | copy-start | bytes 20054020
  143.9 1.4 copy-start.3
  147.5 260.1 %reduce-scatter.7.cloned.1.call-start = ((), (), s32[]{:S(2)}) async-start(), calls=%async_computation.4 | async-start | bytes 18939904
  167.9 273.9 %reduce-scatter.5.cloned.1.call-start = ((), (), s32[]{:S(2)}) async-start(), calls=%async_computation.3 | async-start | bytes 2359296 | tf_op jit(solution)/shard_map/reduce_scatter | solution.py:107
  407.6 35.9 %copy-start.1 = (bf16[256,4096]{1,0:T(8,128)(2,1)S(1)}, bf16[256,4096]{1,0:T(8,128)(2,1)}, u32[]{:S(2)}) copy-start(bf16[256,4096]{1,0:T(8,128)(2,1)} %param.13) | copy-start | bytes 6291460
Sparse Core Ops, SparseCore 0:
  147.6 118.7 all-gather.1
  269.9 115.5 reduce-scatter.6
  407.7 34.0 reduce-scatter.4
where the time goes:
time: 451 us; the launch traced here: 450 us
  waiting for transfers between devices  150 us (33%)
  matrix products  95.4 us (21%)
  other arithmetic  83.4 us (18%)
  local copies, waits for them, and re-layouts  66.4 us (15%)
  loops' own time  31.3 us (7%)
  between operations  17.8 us (4%)
  starting transfers between devices  6.23 us (1%)
    all_gather x1, waiting for transfers between devices, block_product(): piece = lax.all_gather(weight_shard, 'fsdp', axis=0, tiled=True)  98.5 us
    dot_general x16, matrix products, one_shard(): return carry + jnp.dot(columns, block, preferred_element_type=jnp.float32)  85.1 us
    another operation x1, loops' own time, block_product(): return lax.fori_loop(0, shard_count, one_shard, empty)  31.3 us
    ppermute x2, waiting for transfers between devices, passed_along(): lax.ppermute(value, axis, [(source, source + steps) for source in range(l...  29.8 us
    concatenate x1, local copies, waits for them, and re-layouts, migrate(): source = jnp.concatenate([from_left, stacked, from_right], axis=1)  23.1 us
    reduce_scatter x1, waiting for transfers between devices, local(): lax.psum_scatter(block_part.astype(jnp.bfloat16), 'dp', scatter_dimension...  21.3 us
    gather x1, local copies, waits for them, and re-layouts, migrate(): chosen = jnp.take(source, index, axis=1)  17.2 us
    mul x1, other arithmetic, local(): second_next = 0.95 * moved[2] + 0.05 * grad * grad  16.3 us
  transfers between devices with their start and end apart: 5, of which 4 were waited for; matrix products, arithmetic and copies ran while one was open for 33% of the time, Pallas kernels for 0%

commit v1 on v0

--- a/solution.py
+++ b/solution.py
@@ -46,7 +46,9 @@
     )
     row_index = jnp.arange(slot_rows)[:, None]
     empty = jnp.zeros((hidden.shape[0], weight_shard.shape[1]), jnp.float32)
-    piece = lax.all_gather(weight_shard, "fsdp", axis=0, tiled=True)
+    piece = jnp.concatenate(
+        lax.all_to_all(jnp.stack([weight_shard] * lax.axis_size("fsdp")), "fsdp", 0, 0), axis=0
+    )
     shard_count = piece.shape[0] // slot_rows
     blocks = piece.reshape(shard_count, slot_rows, piece.shape[1])
 

time: 451 us -> 794 us (1.76)
  waiting for transfers between devices: 150 us -> 479 us
    all_to_all x0 -> x1, waiting for transfers between devices: none -> 311 us  [block_product(): lax.all_to_all(jnp.stack([weight_shard] * lax.axis_size('fsdp')), 'fsdp',...]
    unnamed x4 -> x3, waiting for transfers between devices: 0.07 us -> 116 us
    all_gather x1 -> x0, waiting for transfers between devices: 98.5 us -> none  [block_product(): piece = lax.all_gather(weight_shard, 'fsdp', axis=0, tiled=True)]
  transfers between devices with their start and end apart: 5 -> 5, of which waited for: 4 -> 5; matrix products, arithmetic and copies ran while one was open for 33% -> 4% of each run, Pallas kernels for 0% -> 0%
where the time goes in v1:
time: 794 us; the launch traced here: 792 us
  waiting for transfers between devices  479 us (60%)
  matrix products  94.1 us (12%)
  other arithmetic  83.2 us (10%)
  local copies, waits for them, and re-layouts  72.7 us (9%)
  loops' own time  31.2 us (4%)
  between operations  18.1 us (2%)
  starting transfers between devices  13.3 us (2%)
    all_to_all x1, waiting for transfers between devices, block_product(): lax.all_to_all(jnp.stack([weight_shard] * lax.axis_size('fsdp')), 'fsdp',...  311 us
    unnamed x3, waiting for transfers between devices  116 us
    dot_general x16, matrix products, one_shard(): return carry + jnp.dot(columns, block, preferred_element_type=jnp.float32)  83.8 us
    another operation x1, loops' own time, block_product(): return lax.fori_loop(0, shard_count, one_shard, empty)  31.2 us
    ppermute x2, waiting for transfers between devices, passed_along(): lax.ppermute(value, axis, [(source, source + steps) for source in range(l...  29.8 us
    concatenate x1, local copies, waits for them, and re-layouts, migrate(): source = jnp.concatenate([from_left, stacked, from_right], axis=1)  23.1 us
    reduce_scatter x1, waiting for transfers between devices, local(): lax.psum_scatter(block_part.astype(jnp.bfloat16), 'dp', scatter_dimension...  22.3 us
    gather x1, local copies, waits for them, and re-layouts, migrate(): chosen = jnp.take(source, index, axis=1)  17.2 us
  transfers between devices with their start and end apart: 5, of which 5 were waited for; matrix products, arithmetic and copies ran while one was open for 4% of the time, Pallas kernels for 0%

profile of v1, /device:TPU:0, one launch (start us, length us, event | category | flops | bytes accessed | tf_op | source)
XLA Modules:
  0.0 792.1 jit_solution(5252869814034566214)
XLA Ops:
  39.6 26.3 %collective-permute-done = bf16[3,58,4096]{2,1,0:T(8,128)(2,1)} collective-permute-done((bf16[3,58,4096]{2,1,0:T(8,128)(2,1)}, bf16[3,58,4096]{2,1,0:T(8,128)(2,1)}, u32[]{:S(2)}, u32[]{:S(2)}) %collective-permute-start) | collective-permute-done | bytes 1425440 | tf_op jit(solution)/shard_map/ppermute | solution.py:11
  75.1 23.1 %copy.39 = f32[3,252,4096]{2,0,1:T(4,128)} copy(f32[3,252,4096]{2,1,0:T(8,128)S(1)} %pad_maximum_fusion) | data formatting | bytes 24772608 | tf_op jit(solution)/shard_map/concatenate | solution.py:27
  98.2 17.2 %gather_fusion = f32[136,3,4096]{2,1,0:T(4,128)} fusion(f32[3,252,4096]{2,0,1:T(4,128)} %copy.39, s32[1024]{0:T(1024)S(1)} %pad_clamp_fusion.1), kind=kCustom, calls=%fused_computation | custom fusion | bytes 13369888 | tf_op jit(solution)/shard_map/jit(_take)/gather | solution.py:38
  115.4 12.2 %select_bitcast_fusion = f32[3,136,4096]{2,0,1:T(4,128)} fusion(f32[136,3,4096]{2,1,0:T(4,128)} %gather_fusion, pred[136]{0:T(512)(128)(4,1)S(1)} %iota_compare_fusion.2, pred[136]{0:T(512)(128)(4,1)S(1)} %compare_and_fusion.1), kind=kLoop, calls=%fused_computation.19 | loop fusion | flops 3342336 | bytes 13369616 | tf_op jit(solution)/shard_map/jit(_where)/select_n | solution.py:39
  127.6 16.3 %slice_multiply_fusion = (f32[1,136,4096]{2,0,1:T(1,128)}, f32[1,136,4096]{2,0,1:T(1,128)S(1)}, f32[1,136,4096]{2,0,1:T(1,128)}) fusion(f32[3,136,4096]{2,0,1:T(4,128)} %select_bitcast_fusion), kind=kLoop, calls=%fused_computation.30 | loop fusion | flops 557056 | bytes 13369344 | tf_op jit(solution)/shard_map/mul | solution.py:133
  146.5 6.4 stack.8
  152.8 7.1 all-to-all-start
  163.1 311.2 %all-to-all-done = bf16[16,136,4096]{2,1,0:T(8,128)(2,1)} async-done(((bf16[16,136,4096]{2,1,0:T(8,128)(2,1)}), bf16[16,136,4096]{2,1,0:T(8,128)(2,1)}, u32[]{:S(2)}, u32[]{:S(2)}) %all-to-all-start) | async-done | bytes 17825824 | tf_op jit(solution)/shard_map/all_to_all | solution.py:50
  474.2 135.9 %while.14 = (s32[]{:T(128)}, f32[256,4096]{1,0:T(8,128)}, s32[16]{0:T(128)S(1)}, bf16[256,1992]{0,1:T(8,128)(2,1)}, s32[16]{0:T(128)S(1)}, /*index=5*/bf16[16,13...) while((s32[]{:T(128)}, f32[256,4096]{1,0:T(8,128)}, s32[16]{0:T(128)S(1)}, ...), condition=%wide.region_9.10_spmd.clone, body=%wide.region_6.9_spmd.clone.sunk | while | flops 287867104 | bytes 9573421 | solution.py:63
  484.8 5.3 convolution_add_fusion.2
  493.4 5.3 convolution_add_fusion.2
  501.9 5.3 convolution_add_fusion.2
  510.5 5.3 convolution_add_fusion.2
  519.1 5.3 convolution_add_fusion.2
  544.8 5.3 convolution_add_fusion.2
  553.4 5.3 convolution_add_fusion.2
  561.9 5.3 convolution_add_fusion.2
  570.5 5.3 convolution_add_fusion.2
  579.1 5.3 convolution_add_fusion.2
  614.2 7.7 gather_fusion.1
  622.0 10.3 %convolution_convert_fusion = bf16[2176,4096]{1,0:T(8,128)(2,1)} fusion(bf16[256,4096]{1,0:T(8,128)(2,1)S(1)} %copy-done, bf16[2176,256]{1,0:T(8,128)(2,1)} %gather_fusion.1, pred[2176]{0:T(1024)(128)(4,1)S(1)} %fusion.35, pred[2176]{0:T(1024)(128)(4,1)S(1)} %compare_and_fusion), kind=kOutput, calls=%fused_computation.16 | convolution fusion | flops 4573429760 | bytes 21041408 | tf_op jit(solution)/shard_map/dot_general | solution.py:123
  632.3 22.3 %reduce-scatter.5.cloned.1.call-done = bf16[256,512]{1,0:T(8,128)(2,1)} async-done(((bf16[256,4096]{1,0:T(8,128)(2,1)}), bf16[256,512]{1,0:T(8,128)(2,1)}) %reduce-scatter.5.cloned.1.call-update) | async-done | bytes 262160 | tf_op jit(solution)/shard_map/reduce_scatter | solution.py:109
  656.4 116.1 %reduce-scatter.7.cloned.1.call-done = bf16[136,4096]{1,0:T(8,128)(2,1)} async-done(((bf16[2176,4096]{1,0:T(8,128)(2,1)}), bf16[136,4096]{1,0:T(8,128)(2,1)}) %reduce-scatter.7.cloned.1.call-update) | async-done | bytes 1114128
  772.5 12.7 %fusion.27 = (f32[1,136,4096]{2,1,0:T(8,128)}, f32[1,136,4096]{2,1,0:T(8,128)}, f32[1,136,4096]{2,1,0:T(8,128)}) fusion(bf16[136,4096]{1,0:T(8,128)(2,1)} %reduce-scatter.7.cloned.1.call-done, f32[1,136,4096]{2,0,1:T(1,128)} %get-tuple-element.204, f32[1,136,4096]{2,0,1:T(1,128)} %get-tuple-element.206, f32[1,136,4096]{2,0,1:T(1,128)} %copy-done.2), kind=kLoop, calls=%fused_computation.48 | loop fusion | flops 7798784 | bytes 14483456 | tf_op jit(solution)/shard_map/broadcast_in_dim | solution.py:135
  (82 shorter events, 100.7 us)
Async XLA Ops:
  7.2 614.8 %copy-start = (bf16[256,4096]{1,0:T(8,128)(2,1)S(1)}, bf16[256,4096]{1,0:T(8,128)(2,1)}, u32[]{:S(2)}) copy-start(bf16[256,4096]{1,0:T(8,128)(2,1)} %param.13) | copy-start | bytes 6291460
  18.3 3.4 copy-start.3
  28.4 37.5 %collective-permute-start = (bf16[3,58,4096]{2,1,0:T(8,128)(2,1)}, bf16[3,58,4096]{2,1,0:T(8,128)(2,1)}, u32[]{:S(2)}, u32[]{:S(2)}) collective-permute-start(bf16[3,58,4096]{2,1,0:T(8,128)(2,1)} %get-tuple-element.207), channel_id=1, source_target_pairs={{0,1},{1,2},{2,3},{3,4},{4,5},{5,6},{6,7},{7,8},{8,9},{9,10},{10,1... | collective-permute-start | bytes 4276232 | tf_op jit(solution)/shard_map/ppermute | solution.py:11
  33.2 38.1 %collective-permute-start.1 = (bf16[3,58,4096]{2,1,0:T(8,128)(2,1)}, bf16[3,58,4096]{2,1,0:T(8,128)(2,1)}, u32[]{:S(2)}, u32[]{:S(2)}) collective-permute-start(bf16[3,58,4096]{2,1,0:T(8,128)(2,1)} %get-tuple-element.208), channel_id=1, source_target_pairs={{1,0},{2,1},{3,2},{4,3},{5,4},{6,5},{7,6},{8,7},{9,8},{10,9},{11,1... | collective-permute-start | bytes 4276232 | tf_op jit(solution)/shard_map/ppermute | solution.py:11
  65.9 7.1 copy-start.1
  143.9 1.4 copy-start.2
  152.8 321.4 %all-to-all-start = ((bf16[16,136,4096]{2,1,0:T(8,128)(2,1)}), bf16[16,136,4096]{2,1,0:T(8,128)(2,1)}, u32[]{:S(2)}, u32[]{:S(2)}) async-start(bf16[16,136,4096]{2,1,0:T(8,128)(2,1)} %stack.8), calls=%async_computation | async-start | bytes 35651584 | tf_op jit(solution)/shard_map/all_to_all | solution.py:50
  159.9 494.7 %reduce-scatter.5.cloned.1.call-start = ((), (), s32[]{:S(2)}) async-start(), calls=%async_computation.3 | async-start | bytes 2359296 | tf_op jit(solution)/shard_map/reduce_scatter | solution.py:109
  613.9 158.6 %reduce-scatter.7.cloned.1.call-start = ((), (), s32[]{:S(2)}) async-start(), calls=%async_computation.4 | async-start | bytes 18939904
Sparse Core Ops, SparseCore 0:
  614.1 40.4 reduce-scatter.4
  658.1 114.4 reduce-scatter.6
